TPU v7x, 256 devices: a whole 4x4x8 slice. The times are simulated.
256 devices in a mesh: head: 16 (over z, core), tail: 16 (over y, x).
Axes of the slice: x: 4, y: 4, z: 8, core: 2. Of those that a mesh axis runs over, the one named last changes fastest.
Arguments:
- head_emb: bfloat16 [131072, 800], P(('head', 'tail')), may hold values from -48 to 48
- head_state: float32 [131072], P(('head', 'tail')), may hold values from 0.01 to 1
- tail_emb: bfloat16 [64, 128, 800], P('tail'), may hold values from -1.5 to 1.5
- tail_state: float32 [64, 128], P('tail'), may hold values from 0.01 to 1
- relation_emb: bfloat16 [1024, 800], replicated, may hold values from -3.5 to 3.5
- head_rows: int32 [1024, 256], P(('head', 'tail')), may hold values from 0 to 511
- relations: int32 [1024, 256], P(('head', 'tail')), may hold values from 0 to 1023
- tail_offsets: int32 [1024, 256], P(('head', 'tail')), may hold values from 0 to 127
- tail_owner: int32 [1024, 1], P(('head', 'tail')), may hold values from 0 to 15; in each aligned block of 4 rows (0 to 3, 4 to 7, ...) at most 2 rows name the same one
- tail_local: int32 [1024], P(('head', 'tail')), may hold values from 0 to 3
- block_count: int32 [256], P(('head', 'tail')), may hold values from 1 to 4, as said below
- neg_blocks: int32 [8], replicated, may hold values from 0 to 63, as said below
Outputs:
- head_new: bfloat16 [131072, 800], P(('head', 'tail'))
- head_state_new: float32 [131072], P(('head', 'tail'))
- tail_new: bfloat16 [64, 128, 800], P('tail')
- tail_state_new: float32 [64, 128], P('tail')
Inputs may be any that keep to these rules, and one draw needn't show every extreme that they name: `tail_owner`: no tail index owns the tail blocks of more than 2 edge block slots of one device, and in some devices one owns exactly 2. `block_count`: some device has all 4 slots live. `neg_blocks`: distinct tail blocks; the last tail block is always among them.
All inputs are finite; a program needn't handle non-finite values.
Results may differ from a plain program's by a relative error of at most 0.0012.
The roundings to bfloat16 on the way count: a program that leaves them out, or rounds other values in their place, can miss the bound.
Values may be sent and summed in bfloat16 or wider, within the bound.
A program may use at most 128 MiB of HBM per device.

v0:
```python
import math
import jax
import jax.numpy as jnp
from jax import lax
from jax.sharding import PartitionSpec as P

LEARN_RATE = 0.3


def complex_product(left, right):
    half_width = left.shape[-1] // 2
    left_re, left_im = (left[..., :half_width], left[..., half_width:])
    right_re, right_im = (right[..., :half_width], right[..., half_width:])
    return jnp.concatenate(
        [left_re * right_re - left_im * right_im, left_re * right_im + left_im * right_re], axis=-1
    )


def conj_product(left, right):
    half_width = left.shape[-1] // 2
    left_re, left_im = (left[..., :half_width], left[..., half_width:])
    right_re, right_im = (right[..., :half_width], right[..., half_width:])
    return jnp.concatenate(
        [left_re * right_re + left_im * right_im, left_im * right_re - left_re * right_im], axis=-1
    )


def row_adagrad(embedding, adagrad_state, gradient):
    state_next = adagrad_state + jnp.mean(gradient * gradient, axis=-1)
    updated = (
        embedding.astype(jnp.float32) - LEARN_RATE * gradient / jnp.sqrt(state_next)[..., None]
    )
    return (updated.astype(jnp.bfloat16), state_next)


def head_sum(tail_grad):
    return lax.psum(tail_grad, "head")


def per_device(
    head_emb,
    head_state,
    tail_emb,
    tail_state,
    relation_emb,
    head_rows,
    relations,
    tail_offsets,
    tail_owner,
    tail_local,
    block_count,
    neg_blocks,
):
    block_total = tail_local.shape[0]
    edge_count = head_rows.shape[1]
    row_width = head_emb.shape[1]
    span_rows = tail_emb.shape[1]
    owned_blocks = tail_emb.shape[0]
    peer_count = lax.axis_size("tail")
    tail_rank = lax.axis_index("tail")
    capacity = max(2, (2 * block_total + peer_count - 1) // peer_count)
    owner_rank = tail_owner[:, 0]
    positions = jnp.arange(block_total, dtype=jnp.int32)
    same_owner = owner_rank[:, None] == owner_rank[None, :]
    earlier = positions[None, :] < positions[:, None]
    slot_index = jnp.sum((same_owner & earlier).astype(jnp.int32), axis=1)
    slot_place = owner_rank * capacity + slot_index
    global_block = owner_rank * owned_blocks + tail_local
    partition = lax.all_gather(tail_emb, "tail", axis=0, tiled=True)
    chosen = jnp.take(partition, global_block, axis=0)
    mine_ids = neg_blocks - tail_rank * owned_blocks
    is_mine = (mine_ids >= 0) & (mine_ids < owned_blocks)
    own_negs = jnp.where(
        is_mine[:, None, None],
        jnp.take(tail_emb, jnp.clip(mine_ids, 0, owned_blocks - 1), axis=0),
        jnp.zeros((), jnp.bfloat16),
    )
    negatives = lax.psum(own_negs.astype(jnp.float32).astype(jnp.bfloat16), "tail").reshape(
        -1, row_width
    )
    total_edges = block_total * edge_count
    flat_rows = head_rows.reshape(-1)
    block_of = jnp.arange(total_edges, dtype=jnp.int32) // edge_count
    live_mask = (block_of < block_count[0]).astype(jnp.float32)
    tail_index = block_of * span_rows + tail_offsets.reshape(-1)
    tail_vectors = jnp.take(chosen.reshape(-1, row_width), tail_index, axis=0)
    relation_vectors = jnp.take(relation_emb, relations.reshape(-1), axis=0)
    head_vectors = jnp.take(head_emb, flat_rows, axis=0)
    query = complex_product(
        head_vectors.astype(jnp.float32), relation_vectors.astype(jnp.float32)
    ).astype(jnp.bfloat16)
    per_group = math.gcd(block_total, max(1, 512 // edge_count))
    group_rows = per_group * edge_count
    group_count = total_edges // group_rows

    def grouped(values):
        return values.reshape((group_count, group_rows) + values.shape[1:])

    def score_group(neg_total, group_items):
        query_rows, tail_rows, live_rows = group_items
        query_float = query_rows.astype(jnp.float32)
        positive = jnp.sum(query_float * tail_rows.astype(jnp.float32), axis=1)
        negative = lax.dot_general(
            query_rows, negatives, (((1,), (1,)), ((), ())), preferred_element_type=jnp.float32
        )
        largest = jnp.maximum(positive, jnp.max(negative, axis=1))
        pos_exp = jnp.exp(positive - largest)
        neg_exp = jnp.exp(negative - largest[:, None])
        denominator = pos_exp + jnp.sum(neg_exp, axis=1)
        pos_grad = (pos_exp / denominator - 1.0) * live_rows
        neg_grad = (neg_exp / denominator[:, None] * live_rows[:, None]).astype(jnp.bfloat16)
        query_grad = pos_grad[:, None] * tail_rows.astype(jnp.float32) + jnp.dot(
            neg_grad, negatives, preferred_element_type=jnp.float32
        )
        tail_part = pos_grad[:, None] * query_float
        neg_total = neg_total + lax.dot_general(
            neg_grad, query_rows, (((0,), (0,)), ((), ())), preferred_element_type=jnp.float32
        )
        return (neg_total, (query_grad, tail_part))

    neg_start = jnp.zeros((negatives.shape[0], row_width), jnp.float32)
    neg_part, (query_grad, tail_part) = lax.scan(
        score_group, neg_start, (grouped(query), grouped(tail_vectors), grouped(live_mask))
    )
    query_grad = query_grad.reshape(total_edges, row_width)
    tail_part = tail_part.reshape(total_edges, row_width)
    head_grad = (
        jnp.zeros(head_emb.shape, jnp.float32)
        .at[flat_rows]
        .add(conj_product(query_grad, relation_vectors.astype(jnp.float32)))
    )
    block_grad = (
        jnp.zeros((block_total * span_rows, row_width), jnp.float32)
        .at[tail_index]
        .add(tail_part)
        .astype(jnp.bfloat16)
    )
    outgoing = (
        jnp.zeros((peer_count * capacity, span_rows, row_width), jnp.bfloat16)
        .at[slot_place]
        .set(block_grad.reshape(block_total, span_rows, row_width))
    )
    outgoing = outgoing.reshape(peer_count, capacity, span_rows, row_width)
    slot_ids = (
        jnp.zeros((peer_count * capacity,), jnp.int32)
        .at[slot_place]
        .set(tail_local)
        .reshape(peer_count, capacity)
    )
    incoming, incoming_ids = (
        lax.all_to_all(outgoing, "tail", split_axis=0, concat_axis=0, tiled=True),
        lax.all_to_all(slot_ids, "tail", split_axis=0, concat_axis=0, tiled=True),
    )
    which_block = (
        incoming_ids.reshape(-1)[:, None] == jnp.arange(owned_blocks, dtype=jnp.int32)[None, :]
    ).astype(jnp.bfloat16)
    tail_grad = lax.dot_general(
        which_block,
        incoming.reshape(peer_count * capacity, span_rows * row_width),
        (((0,), (0,)), ((), ())),
        preferred_element_type=jnp.float32,
    )
    neg_weights = (
        (mine_ids[:, None] == jnp.arange(owned_blocks, dtype=jnp.int32)[None, :]) & is_mine[:, None]
    ).astype(jnp.float32)
    neg_all = lax.psum(neg_part, ("head", "tail"))
    tail_total = head_sum(tail_grad) + lax.dot_general(
        neg_weights,
        neg_all.reshape(neg_weights.shape[0], span_rows * row_width),
        (((0,), (0,)), ((), ())),
        precision=lax.Precision.HIGHEST,
        preferred_element_type=jnp.float32,
    )
    head_updated, head_state_updated = row_adagrad(head_emb, head_state, head_grad)
    tail_updated, tail_state_updated = row_adagrad(
        tail_emb, tail_state, tail_total.reshape(owned_blocks, span_rows, row_width)
    )
    return (head_updated, head_state_updated, tail_updated, tail_state_updated)


def solution(mesh):
    placed = (
        P(("head", "tail"), None),
        P(("head", "tail")),
        P("tail", None, None),
        P("tail", None),
        P(),
        P(("head", "tail"), None),
        P(("head", "tail"), None),
        P(("head", "tail"), None),
        P(("head", "tail"), None),
        P(("head", "tail")),
        P(("head", "tail")),
        P(),
    )
    return jax.shard_map(
        per_device,
        mesh=mesh,
        in_specs=placed,
        out_specs=(
            P(("head", "tail"), None),
            P(("head", "tail")),
            P("tail", None, None),
            P("tail", None),
        ),
        check_vma=False,
    )
```

profile of v0, /device:TPU:1, one launch (start us, length us, event | category | flops | bytes accessed | tf_op | source)
XLA Modules:
  0.0 729.9 jit_solution(752198037437776522)
XLA Ops:
  10.9 7.6 %all-to-all-start = ((s32[16,1,2]{2,1,0:T(1,128)}), s32[16,1,2]{2,1,0:T(1,128)S(1)}, u32[]{:S(2)}, u32[]{:S(2)}) async-start(s32[16,1,2]{2,1,0:T(1,128)} %bitcast.13), calls=%async_computation | async-start | bytes 16384 | tf_op jit(solution)/shard_map/all_to_all | solution.py:152
  29.3 5.3 gather_fusion.3
  34.5 5.3 gather_fusion
  48.7 62.8 %all-gather.2.cloned.1.call-done = bf16[64,128,800]{1,2,0:T(8,128)(2,1)} async-done(((bf16[4,128,800]{1,2,0:T(8,128)(2,1)}), bf16[64,128,800]{1,2,0:T(8,128)(2,1)}) %all-gather.2.cloned.1.call-update) | async-done | bytes 13107216 | tf_op jit(solution)/shard_map/all_gather | solution.py:69
  111.5 5.4 gather_fusion.2
  119.6 5.3 gather_fusion.4
  131.6 81.5 %all-reduce.4.cloned.1.call-done = bf16[1024,800]{1,0:T(8,128)(2,1)} async-done(((bf16[1024,800]{1,0:T(8,128)(2,1)}), bf16[1024,800]{1,0:T(8,128)(2,1)}) %all-reduce.4.cloned.1.call-update) | async-done | bytes 1638416 | tf_op jit(solution)/shard_map/psum | solution.py:78
  213.2 30.7 %while.17 = (s32[]{:T(128)}, f32[1024,800]{0,1:T(8,128)}, f32[2,512,800]{1,2,0:T(8,128)}, f32[2,512,800]{1,2,0:T(8,128)}, bf16[2,512,800]{1,2,0:T(8,128)(2,1)S(1...) while((s32[]{:T(128)}, f32[1024,800]{0,1:T(8,128)}, ...), condition=%wide.region_5.7_spmd.clone, body=%wide.region_1.6_spmd.clone.sunk | while | flops 2527675904 | bytes 74365712 | solution.py:122
  223.6 4.5 select_add_fusion.2
  238.4 5.4 select_add_fusion.2
  248.2 10.8 %scatter_custom_fusion.2 = f32[512,800]{1,0:T(8,128)S(1)} fusion(s32[1024]{0:T(1024)S(1)} %bitcast.112, f32[1024,800]{1,0:T(8,128)} %bitcast.92, f32[]{:T(128)} %constant.133.clone.1), kind=kCustom, calls=%fused_computation.49 | custom fusion | flops 819200 | bytes 1638912 | tf_op jit(solution)/shard_map/scatter-add | solution.py:135
  268.1 4.6 all-to-all-start.1
  272.8 4.9 copy.92
  277.7 6.1 reshape.276
  287.4 4.4 copy.85
  291.8 75.6 %all-to-all-done.1 = bf16[16,2,128,800]{2,3,1,0:T(8,128)(2,1)} async-done(((bf16[16,2,128,800]{2,3,1,0:T(8,128)(2,1)}), bf16[16,2,128,800]{2,3,1,0:T(8,128)(2,1)}, u32[]{:S(2)}, u32[]{:S(2)}) %all-to-all-start.1) | async-done | bytes 6553632 | tf_op jit(solution)/shard_map/all_to_all | solution.py:151
  367.4 11.0 %copy.91 = bf16[16,2,128,800]{3,2,1,0:T(8,128)(2,1)} copy(bf16[16,2,128,800]{2,3,1,0:T(8,128)(2,1)} %all-to-all-done.1) | data formatting | bytes 13107200 | tf_op jit(solution)/shard_map/all_to_all | solution.py:151
  378.5 13.6 %reshape.275 = bf16[32,102400]{1,0:T(8,128)(2,1)} reshape(bf16[16,2,128,800]{3,2,1,0:T(8,128)(2,1)} %copy.91) | data formatting | bytes 13107200 | tf_op jit(solution)/shard_map/reshape | solution.py:159
  392.1 5.1 fusion.20
  397.3 6.6 multiply_add_fusion
  403.9 10.9 %scatter_custom_fusion = f32[512,800]{1,0:T(8,128)S(1)} fusion(s32[1024]{0:T(1024)S(1)} %bitcast.113, f32[1024,400]{1,0:T(8,128)} %get-tuple-element.225, f32[]{:T(128)} %constant.164, f32[1024,400]{1,0:T(8,128)} %get-tuple-element.224, f32[]{:T(128)} %constant.133.clone.1), kind=kCustom, calls=%fused_computation.32 | custom fusion | flops 1638400 | bytes 4915208 | tf_op jit(solution)/shard_map/scatter-add | solution.py:130
  419.1 172.2 %all-reduce.8.cloned.1.call-done = f32[8,102400]{1,0:T(8,128)} async-done(((f32[8,102400]{1,0:T(8,128)}), f32[8,102400]{1,0:T(8,128)}) %all-reduce.8.cloned.1.call-update) | async-done | bytes 3276816 | tf_op jit(solution)/shard_map/psum | solution.py:166
  591.3 116.5 %all-reduce.6.cloned.1.call-done = f32[4,102400]{1,0:T(4,128)} async-done(((f32[4,102400]{1,0:T(4,128)}), f32[4,102400]{1,0:T(4,128)}) %all-reduce.6.cloned.1.call-update) | async-done | bytes 1638416 | tf_op jit(solution)/shard_map/psum | solution.py:37
  707.9 5.1 broadcast_multiply_fusion
  (133 shorter events, 84.3 us)
Async XLA Ops:
  7.2 12.1 %copy-start.3 = (bf16[4,128,800]{1,2,0:T(8,128)(2,1)S(1)}, bf16[4,128,800]{1,2,0:T(8,128)(2,1)}, u32[]{:S(2)}) copy-start(bf16[4,128,800]{1,2,0:T(8,128)(2,1)} %param.18) | copy-start | bytes 2457604
  7.2 104.3 %all-gather.2.cloned.1.call-start = ((), (), s32[]{:S(2)}) async-start(), calls=%async_computation.3 | async-start | bytes 13926400 | tf_op jit(solution)/shard_map/all_gather | solution.py:69
  10.9 257.2 %all-to-all-start = ((s32[16,1,2]{2,1,0:T(1,128)}), s32[16,1,2]{2,1,0:T(1,128)S(1)}, u32[]{:S(2)}, u32[]{:S(2)}) async-start(s32[16,1,2]{2,1,0:T(1,128)} %bitcast.13), calls=%async_computation | async-start | bytes 16384 | tf_op jit(solution)/shard_map/all_to_all | solution.py:152
  18.5 194.7 %all-reduce.4.cloned.1.call-start = ((), (), s32[]{:S(2)}) async-start(), calls=%async_computation.2 | async-start | bytes 3670016 | tf_op jit(solution)/shard_map/psum | solution.py:78
  21.5 3.8 copy-start.12
  21.5 3.9 copy-start.15
  21.5 3.9 copy-start.16
  21.5 3.9 copy-start.9
  26.1 3.1 copy-start.10
  44.2 3.1 copy-start.11
  213.2 3.1 copy-start.2
  213.2 3.9 copy-start.17
  216.2 4.1 copy-start
  216.2 2.7 copy-start.7
  228.1 3.1 copy-start.2
  228.1 3.9 copy-start.17
  231.1 4.1 copy-start
  231.1 2.7 copy-start.7
  268.1 99.3 %all-to-all-start.1 = ((bf16[16,2,128,800]{2,3,1,0:T(8,128)(2,1)}), bf16[16,2,128,800]{2,3,1,0:T(8,128)(2,1)}, u32[]{:S(2)}, u32[]{:S(2)}) async-start(bf16[16,2,128,800]{2,3,1,0:T(8,128)(2,1)} %bitcast.86), calls=%async_computation.1 | async-start | bytes 13107200 | tf_op jit(solution)/shard_map/all_to_all | solution.py:151
  272.7 318.6 %all-reduce.8.cloned.1.call-start = ((), (), s32[]{:S(2)}) async-start(), calls=%async_computation.5 | async-start | bytes 6553600 | tf_op jit(solution)/shard_map/psum | solution.py:166
  283.7 424.1 %all-reduce.6.cloned.1.call-start = ((), (), s32[]{:S(2)}) async-start(), calls=%async_computation.4 | async-start | bytes 3276800 | tf_op jit(solution)/shard_map/psum | solution.py:37
  403.9 11.1 %copy-start.13 = (f32[512]{0:T(512)S(1)}, f32[512]{0:T(512)}, u32[]{:S(2)}) copy-start(f32[512]{0:T(512)} %param.17) | copy-start | bytes 6148
  716.1 3.1 copy-start.14
  716.2 3.7 copy-start.5
  (5 other events, 8.4 us)
Sparse Core Ops, SparseCore 0:
  10.4 101.0 all-gather.1
  114.9 98.2 all-reduce.3
  283.9 307.4 all-reduce.7
  593.6 114.2 all-reduce.5
where the time goes:
time: 731 us; the launch traced here: 730 us
  waiting for transfers between devices  509 us (70%)
  local copies, waits for them, and re-layouts  111 us (15%)
  other arithmetic  52.5 us (7%)
  matrix products  29.1 us (4%)
  between operations  14.8 us (2%)
  starting transfers between devices  12.4 us (2%)
    psum x1, waiting for transfers between devices, per_device(): neg_all = lax.psum(neg_part, ('head', 'tail'))  172 us
    psum x1, waiting for transfers between devices, head_sum(): return lax.psum(tail_grad, 'head')  117 us
    psum x1, waiting for transfers between devices, per_device(): lax.psum(own_negs.astype(jnp.float32).astype(jnp.bfloat16), 'tail')  81.5 us
    all_to_all x1, waiting for transfers between devices, per_device(): lax.all_to_all(outgoing, 'tail', split_axis=0, concat_axis=0, tiled=True)  75.6 us
    all_gather x1, waiting for transfers between devices, per_device(): partition = lax.all_gather(tail_emb, 'tail', axis=0, tiled=True)  62.8 us
  transfers between devices with their start and end apart: 6, of which 5 were waited for; matrix products, arithmetic and copies ran while one was open for 23% of the time, Pallas kernels for 0%

commit v1 on v0

--- a/solution.py
+++ b/solution.py
@@ -5,6 +5,19 @@
 from jax.sharding import PartitionSpec as P
 
 LEARN_RATE = 0.3
+
+
+def collect(x, axis, dim):
+    ways = lax.axis_size(axis)
+    up = [(d, (d + 1) % ways) for d in range(ways)]
+    down = [(d, (d - 1) % ways) for d in range(ways)]
+    earlier, later = ([x], [x])
+    for _ in range(ways // 2):
+        earlier.append(lax.ppermute(earlier[-1], axis, up))
+    for _ in range((ways - 1) // 2):
+        later.append(lax.ppermute(later[-1], axis, down))
+    line = jnp.concatenate([*earlier[::-1], *later[1:]], axis=dim)
+    return jnp.roll(line, (lax.axis_index(axis) - ways // 2) * x.shape[dim], axis=dim)
 
 
 def complex_product(left, right):
@@ -66,7 +79,7 @@
     slot_index = jnp.sum((same_owner & earlier).astype(jnp.int32), axis=1)
     slot_place = owner_rank * capacity + slot_index
     global_block = owner_rank * owned_blocks + tail_local
-    partition = lax.all_gather(tail_emb, "tail", axis=0, tiled=True)
+    partition = collect(tail_emb, "tail", 0)
     chosen = jnp.take(partition, global_block, axis=0)
     mine_ids = neg_blocks - tail_rank * owned_blocks
     is_mine = (mine_ids >= 0) & (mine_ids < owned_blocks)

time: 731 us -> 773 us (1.057); the launches traced: 730 us -> 763 us
  starting transfers between devices: 12.4 us -> 50.5 us
  waiting for transfers between devices: 509 us -> 475 us
  local copies, waits for them, and re-layouts: 111 us -> 143 us
    ppermute x0 -> x15, waiting for transfers between devices: none -> 86.6 us  [the longest x8 64.1 us: collect(): earlier.append(lax.ppermute(earlier[-1], axis, up))]
    all_gather x1 -> x0, waiting for transfers between devices: 62.8 us -> none  [per_device(): partition = lax.all_gather(tail_emb, 'tail', axis=0, tiled=True)]
    psum x1, waiting for transfers between devices: 81.5 us -> 23.3 us  [per_device(): lax.psum(own_negs.astype(jnp.float32).astype(jnp.bfloat16), 'tail')]
    ppermute x0 -> x15, starting transfers between devices: none -> 37.1 us  [the longest x7 34.8 us: collect(): later.append(lax.ppermute(later[-1], axis, down))]
    unnamed x38 -> x81, local copies, waits for them, and re-layouts: 14.2 us -> 38.8 us
  transfers between devices with their start and end apart: 6 -> 20, of which waited for: 5 -> 14; matrix products, arithmetic and copies ran while one was open for 23% -> 26% of each run, Pallas kernels for 0% -> 0%
where the time goes in v1:
time: 773 us; the launch traced here: 763 us
  waiting for transfers between devices  475 us (61%)
  local copies, waits for them, and re-layouts  143 us (18%)
  other arithmetic  50.6 us (7%)
  starting transfers between devices  50.5 us (7%)
  matrix products  29 us (4%)
  between operations  15.3 us (2%)
    psum x1, waiting for transfers between devices, per_device(): neg_all = lax.psum(neg_part, ('head', 'tail'))  173 us
    psum x1, waiting for transfers between devices, head_sum(): return lax.psum(tail_grad, 'head')  117 us
    all_to_all x1, waiting for transfers between devices, per_device(): lax.all_to_all(outgoing, 'tail', split_axis=0, concat_axis=0, tiled=True)  75 us
    ppermute x8, waiting for transfers between devices, collect(): earlier.append(lax.ppermute(earlier[-1], axis, up))  64.1 us
    unnamed x81, local copies, waits for them, and re-layouts  38.8 us
    ppermute x7, starting transfers between devices, collect(): later.append(lax.ppermute(later[-1], axis, down))  34.8 us
    psum x1, waiting for transfers between devices, per_device(): lax.psum(own_negs.astype(jnp.float32).astype(jnp.bfloat16), 'tail')  23.3 us
    ppermute x7, waiting for transfers between devices, collect(): later.append(lax.ppermute(later[-1], axis, down))  22.5 us
  transfers between devices with their start and end apart: 20, of which 14 were waited for; matrix products, arithmetic and copies ran while one was open for 26% of the time, Pallas kernels for 0%

profile of v1, /device:TPU:1, one launch (start us, length us, event | category | flops | bytes accessed | tf_op | source)
XLA Modules:
  0.0 762.8 jit_solution(9563556101656185148)
XLA Ops:
  9.3 20.0 %collective-permute-done = bf16[4,128,800]{1,2,0:T(8,128)(2,1)S(1)} collective-permute-done((bf16[4,128,800]{1,2,0:T(8,128)(2,1)}, bf16[4,128,800]{1,2,0:T(8,128)(2,1)S(1)}, u32[]{:S(2)}, u32[]{:S(2)}) %collective-permute-start) | collective-permute-done | bytes 819232 | tf_op jit(solution)/shard_map/ppermute | solution.py:16
  34.1 15.2 %collective-permute-done.1 = bf16[4,128,800]{1,2,0:T(8,128)(2,1)S(1)} collective-permute-done((bf16[4,128,800]{1,2,0:T(8,128)(2,1)S(1)}, bf16[4,128,800]{1,2,0:T(8,128)(2,1)S(1)}, u32[]{:S(2)}, u32[]{:S(2)}) %collective-permute-start.1) | collective-permute-done | bytes 819232 | tf_op jit(solution)/shard_map/ppermute | solution.py:16
  55.6 13.1 %collective-permute-done.2 = bf16[4,128,800]{1,2,0:T(8,128)(2,1)} collective-permute-done((bf16[4,128,800]{1,2,0:T(8,128)(2,1)S(1)}, bf16[4,128,800]{1,2,0:T(8,128)(2,1)}, u32[]{:S(2)}, u32[]{:S(2)}) %collective-permute-start.2) | collective-permute-done | bytes 819232 | tf_op jit(solution)/shard_map/ppermute | solution.py:16
  81.1 6.2 collective-permute-done.3
  88.6 8.6 %all-to-all-start = ((s32[16,1,2]{2,1,0:T(1,128)}), s32[16,1,2]{2,1,0:T(1,128)S(1)}, u32[]{:S(2)}, u32[]{:S(2)}) async-start(s32[16,1,2]{2,1,0:T(1,128)} %bitcast.13), calls=%async_computation | async-start | bytes 16384 | tf_op jit(solution)/shard_map/all_to_all | solution.py:165
  102.1 5.4 collective-permute-done.4
  133.1 5.5 collective-permute-done.12
  148.1 14.5 %collective-permute-done.13 = bf16[4,128,800]{1,2,0:T(8,128)(2,1)S(1)} collective-permute-done((bf16[4,128,800]{1,2,0:T(8,128)(2,1)}, bf16[4,128,800]{1,2,0:T(8,128)(2,1)S(1)}, u32[]{:S(2)}, u32[]{:S(2)}) %collective-permute-start.13) | collective-permute-done | bytes 819232 | tf_op jit(solution)/shard_map/ppermute | solution.py:18
  162.5 5.5 collective-permute-start.14
  196.3 5.6 constant_dynamic-slice_fusion.1
  202.0 5.5 gather_fusion.2
  221.9 23.3 %all-reduce.4.cloned.1.call-done = bf16[1024,800]{1,0:T(8,128)(2,1)} async-done(((bf16[1024,800]{1,0:T(8,128)(2,1)}), bf16[1024,800]{1,0:T(8,128)(2,1)}) %all-reduce.4.cloned.1.call-update) | async-done | bytes 1638416 | tf_op jit(solution)/shard_map/psum | solution.py:91
  245.3 30.6 %while.17 = (s32[]{:T(128)}, f32[1024,800]{0,1:T(8,128)}, f32[2,512,800]{1,2,0:T(8,128)}, f32[2,512,800]{1,2,0:T(8,128)}, bf16[2,512,800]{1,2,0:T(8,128)(2,1)S(1...) while((s32[]{:T(128)}, f32[1024,800]{0,1:T(8,128)}, ...), condition=%wide.region_5.7_spmd.clone, body=%wide.region_1.0_spmd.clone.sunk | while | flops 2527675904 | bytes 74365712 | solution.py:135
  270.5 5.4 select_add_fusion.2
  280.3 10.7 %scatter_custom_fusion.2 = f32[512,800]{1,0:T(8,128)S(1)} fusion(s32[1024]{0:T(1024)S(1)} %bitcast.112, f32[1024,800]{1,0:T(8,128)} %bitcast.92, f32[]{:T(128)} %constant.153.clone.1), kind=kCustom, calls=%fused_computation.49 | custom fusion | flops 819200 | bytes 1638912 | tf_op jit(solution)/shard_map/scatter-add | solution.py:148
  304.6 5.3 copy.92
  309.9 6.0 reshape.276
  324.0 75.0 %all-to-all-done.1 = bf16[16,2,128,800]{2,3,1,0:T(8,128)(2,1)} async-done(((bf16[16,2,128,800]{2,3,1,0:T(8,128)(2,1)}), bf16[16,2,128,800]{2,3,1,0:T(8,128)(2,1)}, u32[]{:S(2)}, u32[]{:S(2)}) %all-to-all-start.1) | async-done | bytes 6553632 | tf_op jit(solution)/shard_map/all_to_all | solution.py:164
  399.1 11.0 %copy.91 = bf16[16,2,128,800]{3,2,1,0:T(8,128)(2,1)} copy(bf16[16,2,128,800]{2,3,1,0:T(8,128)(2,1)} %all-to-all-done.1) | data formatting | bytes 13107200 | tf_op jit(solution)/shard_map/all_to_all | solution.py:164
  410.1 13.6 %reshape.275 = bf16[32,102400]{1,0:T(8,128)(2,1)} reshape(bf16[16,2,128,800]{3,2,1,0:T(8,128)(2,1)} %copy.91) | data formatting | bytes 13107200 | tf_op jit(solution)/shard_map/reshape | solution.py:172
  428.9 6.7 multiply_add_fusion
  435.5 11.0 %scatter_custom_fusion = f32[512,800]{1,0:T(8,128)S(1)} fusion(s32[1024]{0:T(1024)S(1)} %bitcast.113, f32[1024,400]{1,0:T(8,128)} %get-tuple-element.225, f32[]{:T(128)} %constant.186, f32[1024,400]{1,0:T(8,128)} %get-tuple-element.224, f32[]{:T(128)} %constant.153.clone.1), kind=kCustom, calls=%fused_computation.32 | custom fusion | flops 1638400 | bytes 4915208 | tf_op jit(solution)/shard_map/scatter-add | solution.py:143
  450.9 173.0 %all-reduce.8.cloned.1.call-done = f32[8,102400]{1,0:T(8,128)} async-done(((f32[8,102400]{1,0:T(8,128)}), f32[8,102400]{1,0:T(8,128)}) %all-reduce.8.cloned.1.call-update) | async-done | bytes 3276816 | tf_op jit(solution)/shard_map/psum | solution.py:179
  623.9 116.7 %all-reduce.6.cloned.1.call-done = f32[4,102400]{1,0:T(4,128)} async-done(((f32[4,102400]{1,0:T(4,128)}), f32[4,102400]{1,0:T(4,128)}) %all-reduce.6.cloned.1.call-update) | async-done | bytes 1638416 | tf_op jit(solution)/shard_map/psum | solution.py:50
  (204 shorter events, 184.4 us)
Async XLA Ops:
  7.2 238.1 %all-reduce.4.cloned.1.call-start = ((), (), s32[]{:S(2)}) async-start(), calls=%async_computation.2 | async-start | bytes 3670016 | tf_op jit(solution)/shard_map/psum | solution.py:91
  7.2 22.1 %collective-permute-start = (bf16[4,128,800]{1,2,0:T(8,128)(2,1)}, bf16[4,128,800]{1,2,0:T(8,128)(2,1)S(1)}, u32[]{:S(2)}, u32[]{:S(2)}) collective-permute-start(bf16[4,128,800]{1,2,0:T(8,128)(2,1)} %param.18), channel_id=1, source_target_pairs={{0,1},{1,2},{2,3},{3,4},{4,5},{5,6},{6,7},{7,8},{8,9},{9,10},{10,1... | collective-permute-start | bytes 2457608 | tf_op jit(solution)/shard_map/ppermute | solution.py:16
  29.4 42.8 %copy-start.7 = (bf16[4,128,800]{1,2,0:T(8,128)(2,1)}, bf16[4,128,800]{1,2,0:T(8,128)(2,1)S(1)}, u32[]{:S(2)}) copy-start(bf16[4,128,800]{1,2,0:T(8,128)(2,1)S(1)} %collective-permute-done) | copy-start | bytes 2457604
  29.4 20.0 %collective-permute-start.1 = (bf16[4,128,800]{1,2,0:T(8,128)(2,1)S(1)}, bf16[4,128,800]{1,2,0:T(8,128)(2,1)S(1)}, u32[]{:S(2)}, u32[]{:S(2)}) collective-permute-start(bf16[4,128,800]{1,2,0:T(8,128)(2,1)S(1)} %collective-permute-done), channel_id=1, source_target_pairs={{0,1},{1,2},{2,3},{3,4},{4,5},{5,6},{6,7},{7,8},{8,9},{9,10},{10,1... | collective-permute-start | bytes 2457608 | tf_op jit(solution)/shard_map/ppermute | solution.py:16
  29.4 21.4 %collective-permute-start.8 = (bf16[4,128,800]{1,2,0:T(8,128)(2,1)}, bf16[4,128,800]{1,2,0:T(8,128)(2,1)S(1)}, u32[]{:S(2)}, u32[]{:S(2)}) collective-permute-start(bf16[4,128,800]{1,2,0:T(8,128)(2,1)} %param.18), channel_id=1, source_target_pairs={{0,15},{1,0},{2,1},{3,2},{4,3},{5,4},{6,5},{7,6},{8,7},{9,8},{10,9... | collective-permute-start | bytes 2457608 | tf_op jit(solution)/shard_map/ppermute | solution.py:18
  49.4 19.3 %collective-permute-start.2 = (bf16[4,128,800]{1,2,0:T(8,128)(2,1)S(1)}, bf16[4,128,800]{1,2,0:T(8,128)(2,1)}, u32[]{:S(2)}, u32[]{:S(2)}) collective-permute-start(bf16[4,128,800]{1,2,0:T(8,128)(2,1)S(1)} %collective-permute-done.1), channel_id=1, source_target_pairs={{0,1},{1,2},{2,3},{3,4},{4,5},{5,6},{6,7},{7,8},{8,9},{9,10},{10,1... | collective-permute-start | bytes 2457608 | tf_op jit(solution)/shard_map/ppermute | solution.py:16
  50.8 25.5 %collective-permute-start.9 = (bf16[4,128,800]{1,2,0:T(8,128)(2,1)S(1)}, bf16[4,128,800]{1,2,0:T(8,128)(2,1)}, u32[]{:S(2)}, u32[]{:S(2)}) collective-permute-start(bf16[4,128,800]{1,2,0:T(8,128)(2,1)S(1)} %collective-permute-done.8), channel_id=1, source_target_pairs={{0,15},{1,0},{2,1},{3,2},{4,3},{5,4},{6,5},{7,6},{8,7},{9,8},{10,9... | collective-permute-start | bytes 2457608 | tf_op jit(solution)/shard_map/ppermute | solution.py:18
  68.7 18.6 %collective-permute-start.3 = (bf16[4,128,800]{1,2,0:T(8,128)(2,1)}, bf16[4,128,800]{1,2,0:T(8,128)(2,1)}, u32[]{:S(2)}, u32[]{:S(2)}) collective-permute-start(bf16[4,128,800]{1,2,0:T(8,128)(2,1)} %collective-permute-done.2), channel_id=1, source_target_pairs={{0,1},{1,2},{2,3},{3,4},{4,5},{5,6},{6,7},{7,8},{8,9},{9,10},{10,1... | collective-permute-start | bytes 2457608 | tf_op jit(solution)/shard_map/ppermute | solution.py:16
  72.2 25.0 %copy-start.17 = (s32[4,256]{1,0:T(4,128)S(1)}, s32[4,256]{1,0:T(4,128)}, u32[]{:S(2)}) copy-start(s32[4,256]{1,0:T(4,128)} %param.23) | copy-start | bytes 12292
  72.2 25.1 %copy-start.16 = (s32[4,256]{1,0:T(4,128)S(1)}, s32[4,256]{1,0:T(4,128)}, u32[]{:S(2)}) copy-start(s32[4,256]{1,0:T(4,128)} %param.22) | copy-start | bytes 12292
  72.2 35.4 %copy-start.15 = (bf16[512,800]{0,1:T(8,128)(2,1)S(1)}, bf16[512,800]{0,1:T(8,128)(2,1)}, u32[]{:S(2)}) copy-start(bf16[512,800]{0,1:T(8,128)(2,1)} %param.16) | copy-start | bytes 2457604
  76.3 21.1 %collective-permute-start.10 = (bf16[4,128,800]{1,2,0:T(8,128)(2,1)}, bf16[4,128,800]{1,2,0:T(8,128)(2,1)}, u32[]{:S(2)}, u32[]{:S(2)}) collective-permute-start(bf16[4,128,800]{1,2,0:T(8,128)(2,1)} %collective-permute-done.9), channel_id=1, source_target_pairs={{0,15},{1,0},{2,1},{3,2},{4,3},{5,4},{6,5},{7,6},{8,7},{9,8},{10,9... | collective-permute-start | bytes 2457608 | tf_op jit(solution)/shard_map/ppermute | solution.py:18
  87.3 20.2 %collective-permute-start.4 = (bf16[4,128,800]{1,2,0:T(8,128)(2,1)}, bf16[4,128,800]{1,2,0:T(8,128)(2,1)}, u32[]{:S(2)}, u32[]{:S(2)}) collective-permute-start(bf16[4,128,800]{1,2,0:T(8,128)(2,1)} %collective-permute-done.3), channel_id=1, source_target_pairs={{0,1},{1,2},{2,3},{3,4},{4,5},{5,6},{6,7},{7,8},{8,9},{9,10},{10,1... | collective-permute-start | bytes 2457608 | tf_op jit(solution)/shard_map/ppermute | solution.py:16
  88.6 211.3 %all-to-all-start = ((s32[16,1,2]{2,1,0:T(1,128)}), s32[16,1,2]{2,1,0:T(1,128)S(1)}, u32[]{:S(2)}, u32[]{:S(2)}) async-start(s32[16,1,2]{2,1,0:T(1,128)} %bitcast.13), calls=%async_computation | async-start | bytes 16384 | tf_op jit(solution)/shard_map/all_to_all | solution.py:165
  97.4 26.8 %collective-permute-start.11 = (bf16[4,128,800]{1,2,0:T(8,128)(2,1)}, bf16[4,128,800]{1,2,0:T(8,128)(2,1)}, u32[]{:S(2)}, u32[]{:S(2)}) collective-permute-start(bf16[4,128,800]{1,2,0:T(8,128)(2,1)} %collective-permute-done.10), channel_id=1, source_target_pairs={{0,15},{1,0},{2,1},{3,2},{4,3},{5,4},{6,5},{7,6},{8,7},{9,8},{10,9... | collective-permute-start | bytes 2457608 | tf_op jit(solution)/shard_map/ppermute | solution.py:18
  107.5 21.5 %collective-permute-start.5 = (bf16[4,128,800]{1,2,0:T(8,128)(2,1)}, bf16[4,128,800]{1,2,0:T(8,128)(2,1)}, u32[]{:S(2)}, u32[]{:S(2)}) collective-permute-start(bf16[4,128,800]{1,2,0:T(8,128)(2,1)} %collective-permute-done.4), channel_id=1, source_target_pairs={{0,1},{1,2},{2,3},{3,4},{4,5},{5,6},{6,7},{7,8},{8,9},{9,10},{10,1... | collective-permute-start | bytes 2457608 | tf_op jit(solution)/shard_map/ppermute | solution.py:16
  124.2 14.4 %collective-permute-start.12 = (bf16[4,128,800]{1,2,0:T(8,128)(2,1)}, bf16[4,128,800]{1,2,0:T(8,128)(2,1)}, u32[]{:S(2)}, u32[]{:S(2)}) collective-permute-start(bf16[4,128,800]{1,2,0:T(8,128)(2,1)} %collective-permute-done.11), channel_id=1, source_target_pairs={{0,15},{1,0},{2,1},{3,2},{4,3},{5,4},{6,5},{7,6},{8,7},{9,8},{10,9... | collective-permute-start | bytes 2457608 | tf_op jit(solution)/shard_map/ppermute | solution.py:18
  129.0 17.7 %collective-permute-start.6 = (bf16[4,128,800]{1,2,0:T(8,128)(2,1)}, bf16[4,128,800]{1,2,0:T(8,128)(2,1)}, u32[]{:S(2)}, u32[]{:S(2)}) collective-permute-start(bf16[4,128,800]{1,2,0:T(8,128)(2,1)} %collective-permute-done.5), channel_id=1, source_target_pairs={{0,1},{1,2},{2,3},{3,4},{4,5},{5,6},{6,7},{7,8},{8,9},{9,10},{10,1... | collective-permute-start | bytes 2457608 | tf_op jit(solution)/shard_map/ppermute | solution.py:16
  138.6 23.9 %collective-permute-start.13 = (bf16[4,128,800]{1,2,0:T(8,128)(2,1)}, bf16[4,128,800]{1,2,0:T(8,128)(2,1)S(1)}, u32[]{:S(2)}, u32[]{:S(2)}) collective-permute-start(bf16[4,128,800]{1,2,0:T(8,128)(2,1)} %collective-permute-done.12), channel_id=1, source_target_pairs={{0,15},{1,0},{2,1},{3,2},{4,3},{5,4},{6,5},{7,6},{8,7},{9,8},{10,9... | collective-permute-start | bytes 2457608 | tf_op jit(solution)/shard_map/ppermute | solution.py:18
  146.7 22.6 %collective-permute-start.7 = (bf16[4,128,800]{1,2,0:T(8,128)(2,1)}, bf16[4,128,800]{1,2,0:T(8,128)(2,1)S(1)}, u32[]{:S(2)}, u32[]{:S(2)}) collective-permute-start(bf16[4,128,800]{1,2,0:T(8,128)(2,1)} %collective-permute-done.6), channel_id=1, source_target_pairs={{0,1},{1,2},{2,3},{3,4},{4,5},{5,6},{6,7},{7,8},{8,9},{9,10},{10,1... | collective-permute-start | bytes 2457608 | tf_op jit(solution)/shard_map/ppermute | solution.py:16
  162.5 21.6 %collective-permute-start.14 = (bf16[4,128,800]{1,2,0:T(8,128)(2,1)S(1)}, bf16[4,128,800]{1,2,0:T(8,128)(2,1)S(1)}, u32[]{:S(2)}, u32[]{:S(2)}) collective-permute-start(bf16[4,128,800]{1,2,0:T(8,128)(2,1)S(1)} %collective-permute-done.13), channel_id=1, source_target_pairs={{0,15},{1,0},{2,1},{3,2},{4,3},{5,4},{6,5},{7,6},{8,7},{9,8},{10,9... | collective-permute-start | bytes 2457608 | tf_op jit(solution)/shard_map/ppermute | solution.py:18
  299.9 99.2 %all-to-all-start.1 = ((bf16[16,2,128,800]{2,3,1,0:T(8,128)(2,1)}), bf16[16,2,128,800]{2,3,1,0:T(8,128)(2,1)}, u32[]{:S(2)}, u32[]{:S(2)}) async-start(bf16[16,2,128,800]{2,3,1,0:T(8,128)(2,1)} %bitcast.86), calls=%async_computation.1 | async-start | bytes 13107200 | tf_op jit(solution)/shard_map/all_to_all | solution.py:164
  304.5 319.3 %all-reduce.8.cloned.1.call-start = ((), (), s32[]{:S(2)}) async-start(), calls=%async_computation.4 | async-start | bytes 6553600 | tf_op jit(solution)/shard_map/psum | solution.py:179
  315.9 424.6 %all-reduce.6.cloned.1.call-start = ((), (), s32[]{:S(2)}) async-start(), calls=%async_computation.3 | async-start | bytes 3276800 | tf_op jit(solution)/shard_map/psum | solution.py:50
  (25 other events, 135.5 us)
Sparse Core Ops, SparseCore 0:
  76.2 169.0 all-reduce.3
  316.0 307.7 all-reduce.7
  626.2 114.2 all-reduce.5
